TPU v7x, 256 devices: a whole 4x4x8 slice. The times are simulated.
256 devices in a mesh: outer: 16 (over z_hi, y, core), inner: 16 (over x, z_lo).
Axes of the slice: x: 4, y: 4, z: 8 (z_hi: 2, z_lo: 4; z = z_hi * 4 + z_lo), core: 2. Of those that a mesh axis runs over, the one named last changes fastest.
Arguments:
- queries: bfloat16 [32768, 4096], P(('outer', 'inner')), may hold values from -40 to 40
- keys: bfloat16 [32768, 512], P(('outer', 'inner')), may hold values from -4 to 4
- values: bfloat16 [32768, 512], P(('outer', 'inner')), may hold values from -6 to 6
- doc_lengths: int32 [16], replicated, may hold values from 1 to 8192, 32768 in all
Outputs:
- attended: bfloat16 [32768, 4096], P(('outer', 'inner'))
All inputs are finite; a program needn't handle non-finite values.
Results may differ from a plain program's by a relative error of at most 0.005.
Values may be sent and summed in bfloat16 or wider, within the bound.
A program may use at most 256 MiB of HBM per device.

v0:
```python
import jax
import jax.numpy as jnp
from jax import lax
from jax.sharding import PartitionSpec as P

HEADS = 32
GROUPS = 4
HEAD_DIM = 128
OUTER_STEPS = 2


NEGATIVE = -1e30


def from_behind(array, axis, by):
    size = lax.axis_size(axis)
    pairs = [(i, i + by) for i in range(size) if 0 <= i + by < size]
    return lax.ppermute(array, axis, pairs)


def in_one_piece(arrays, axis, dim, along):
    ends, at = ([], 0)
    for a in arrays[:-1]:
        at += a.shape[along]
        ends.append(at)
    both = jnp.concatenate(arrays, axis=along)
    return tuple(jnp.split(lax.all_gather(both, axis, axis=dim, tiled=True), ends, axis=along))


def doc_of(positions, ends):
    return jnp.sum((positions[:, None] >= ends[None, :]).astype(jnp.int32), axis=1)


def tile_update(state, query4, key_rows, value_rows, allowed, scale):
    acc, top, total = state
    scores = (
        jnp.einsum("qghd,kgd->qghk", query4, key_rows, preferred_element_type=jnp.float32) * scale
    )
    scores = jnp.where(allowed[:, None, None, :], scores, NEGATIVE)
    new_top = jnp.maximum(top, jnp.max(scores, axis=3))
    weights = jnp.where(allowed[:, None, None, :], jnp.exp(scores - new_top[:, :, :, None]), 0.0)
    fade = jnp.exp(top - new_top)
    total = total * fade + jnp.sum(weights, axis=3)
    mixed = jnp.einsum(
        "qghk,kgd->qghd",
        weights.astype(jnp.bfloat16),
        value_rows,
        preferred_element_type=jnp.float32,
    )
    acc = acc * fade[:, :, :, None] + mixed
    return (acc, new_top, total)


def attend_tile(state, query4, qpos, qdoc, key_rows, value_rows, kpos, ends, scale):
    kdoc = doc_of(kpos, ends)
    allowed = (
        (kpos[None, :] <= qpos[:, None]) & (kpos[None, :] >= 0) & (kdoc[None, :] == qdoc[:, None])
    )
    return lax.cond(
        jnp.any(allowed),
        lambda carry: tile_update(carry, query4, key_rows, value_rows, allowed, scale),
        lambda carry: carry,
        state,
    )


def attend_rows(state, query4, qpos, qdoc, key_rows, value_rows, kpos, ends, scale):
    count = key_rows.shape[0]
    width = 512
    key_tiles = key_rows.reshape(count // width, width, GROUPS, HEAD_DIM)
    value_tiles = value_rows.reshape(count // width, width, GROUPS, HEAD_DIM)
    pos_tiles = kpos.reshape(count // width, width)

    def visit(carry, item):
        return (
            attend_tile(carry, query4, qpos, qdoc, item[0], item[1], item[2], ends, scale),
            None,
        )

    state, unused = lax.scan(visit, state, (key_tiles, value_tiles, pos_tiles))
    return state


def body(queries, keys, values, doc_lengths):
    tokens = queries.shape[0]
    per_group = HEADS // GROUPS
    scale = HEAD_DIM ** (-0.5)
    n_inner = lax.axis_size("inner")
    outer_index = lax.axis_index("outer")
    inner_index = lax.axis_index("inner")
    block = tokens * n_inner
    ends = jnp.cumsum(doc_lengths)
    query4 = queries.reshape(tokens, GROUPS, per_group, HEAD_DIM)
    qpos = outer_index * block + inner_index * tokens + jnp.arange(tokens, dtype=jnp.int32)
    qdoc = doc_of(qpos, ends)
    fresh = (
        jnp.zeros((tokens, GROUPS, per_group, HEAD_DIM), jnp.float32),
        jnp.full((tokens, GROUPS, per_group), NEGATIVE, jnp.float32),
        jnp.zeros((tokens, GROUPS, per_group), jnp.float32),
    )
    state = fresh
    pair = (keys, values)
    for step in range(OUTER_STEPS + 1):
        if step > 0:
            pair = from_behind((pair[0], pair[1]), "outer", 1)
        root = (outer_index - step) * block

        def fold(carry, piece, start, root=root):
            kpos = root + jnp.arange(piece[0].shape[0], dtype=jnp.int32)
            return attend_rows(carry, query4, qpos, qdoc, piece[0], piece[1], kpos, ends, scale)

        state = fold(state, in_one_piece((pair[0], pair[1]), "inner", 0, 1), jnp.int32(0))
    result = state[0] / state[2][:, :, :, None]
    return result.astype(jnp.bfloat16).reshape(tokens, HEADS * HEAD_DIM)


def solution(mesh):
    in_specs = (
        P(("outer", "inner"), None),
        P(("outer", "inner"), None),
        P(("outer", "inner"), None),
        P(),
    )
    out_specs = P(("outer", "inner"), None)
    return jax.shard_map(body, mesh=mesh, in_specs=in_specs, out_specs=out_specs, check_vma=False)
```

profile of v0, /device:TPU:8, one launch (start us, length us, event | category | flops | bytes accessed | tf_op | source)
XLA Modules:
  0.0 389.0 jit_solution(5147288653553359738)
XLA Ops:
  10.2 3.6 collective-permute-start.1
  19.5 3.6 collective-permute-start.3
  29.9 84.1 %all-gather.4.cloned.1.call-done = bf16[2048,1024]{1,0:T(8,128)(2,1)} async-done(((bf16[128,1024]{1,0:T(8,128)(2,1)}), bf16[2048,1024]{1,0:T(8,128)(2,1)}) %all-gather.4.cloned.1.call-update) | async-done | bytes 4194320 | tf_op jit(solution)/shard_map/all_gather | solution.py:27
  114.0 3.9 fusion.68
  122.0 4.0 %reshape.89 = bf16[4,512,4,128]{3,2,1,0:T(4,128)(2,1)} reshape(bf16[2048,512]{1,0:T(8,128)(2,1)} %get-tuple-element.661) | data formatting | bytes 4194304 | tf_op jit(solution)/shard_map/reshape | solution.py:71
  130.9 15.8 %while.45 = (s32[]{:T(128)}, f32[128,4,8,128]{3,0,2,1:T(8,128)}, f32[128,4,8]{0,2,1:T(8,128)S(1)}, f32[128,4,8]{0,2,1:T(8,128)S(1)}, s32[4,512]{1,0:T(4,128)S(1)...) while((s32[]{:T(128)}, f32[128,4,8,128]{3,0,2,1:T(8,128)}, ...), condition=%wide.region_9.10_spmd.clone, body=%wide.region_2.9_spmd.clone.sunk | while | flops 1102413952 | bytes 48774520 | solution.py:80
  132.6 9.0 %conditional.9 = ((f32[128,4,8,128]{3,0,2,1:T(8,128)}, f32[128,4,8]{0,2,1:T(8,128)S(1)}, f32[128,4,8]{0,2,1:T(8,128)S(1)})) conditional(s32[]{:T(128)} %convert_element_type.71, (f32[128,4,8,128]{3,0,2,1:T(8,128)}, f32[128,4,8]{0,2,1:T(8,128)S(1)}, f32[128,4,8]{0,2,1:T(8,128)S(1)}) %tuple.125, (pred[128,512]{0,1:T(8,128)(4,1)S(1)}, ...), branch_computations={%region_5.5_spmd, %region_6.8_spmd} | conditional | flops 1102061568 | bytes 48693852 | solution.py:59
  136.1 4.2 %bitcast_add_fusion = f32[128,4,8,128]{3,0,2,1:T(8,128)S(1)} fusion(f32[128,4,8,128]{3,0,2,1:T(8,128)S(1)} %copy-done, f32[4,512,128,8]{2,1,3,0:T(8,128)S(1)} %get-tuple-element.652, f32[128,4,8]{0,2,1:T(8,128)S(1)} %max.12, pred[128,512]{0,1:T(8,128)(4,1)S(1)} %get-tuple-element.334, f32[128,4,8]{0,2,1:T(8,128)S(1)} %get-tuple-element.634, ...), kind=kOutput, calls=%fused_computation.10 | convolution fusion | flops 548405248 | bytes 13206016 | tf_op jit(solution)/shard_map/while/body/eval_jaxpr/cond/branch_1_fun/qghk,kgd->qghd/dot_general | solution.py:44
  146.7 73.0 %all-gather.6.cloned.1.call-done = bf16[2048,1024]{1,0:T(8,128)(2,1)} async-done(((bf16[128,1024]{1,0:T(8,128)(2,1)}), bf16[2048,1024]{1,0:T(8,128)(2,1)}) %all-gather.6.cloned.1.call-update) | async-done | bytes 4194320 | tf_op jit(solution)/shard_map/all_gather | solution.py:27
  219.7 3.9 fusion.67
  227.6 4.0 %reshape.91 = bf16[4,512,4,128]{3,2,1,0:T(4,128)(2,1)} reshape(bf16[2048,512]{1,0:T(8,128)(2,1)} %get-tuple-element.659) | data formatting | bytes 4194304 | tf_op jit(solution)/shard_map/reshape | solution.py:71
  235.0 42.5 %while.46 = (s32[]{:T(128)}, f32[128,4,8,128]{3,0,2,1:T(8,128)}, f32[128,4,8]{0,2,1:T(8,128)S(1)}, f32[128,4,8]{0,2,1:T(8,128)S(1)}, s32[4,512]{1,0:T(4,128)S(1)...) while((s32[]{:T(128)}, f32[128,4,8,128]{3,0,2,1:T(8,128)}, ...), condition=%wide.region_17.18_spmd.clone, body=%wide.region_10.17_spmd.clone.sunk | while | flops 1102413952 | bytes 48774520 | solution.py:80
  236.6 9.0 %conditional.10 = ((f32[128,4,8,128]{3,0,2,1:T(8,128)}, f32[128,4,8]{0,2,1:T(8,128)S(1)}, f32[128,4,8]{0,2,1:T(8,128)S(1)})) conditional(s32[]{:T(128)} %convert_element_type.73, (f32[128,4,8,128]{3,0,2,1:T(8,128)}, f32[128,4,8]{0,2,1:T(8,128)S(1)}, f32[128,4,8]{0,2,1:T(8,128)S(1)}) %tuple.130, (pred[128,512]{0,1:T(8,128)(4,1)S(1)}, ...), branch_computations={%region_13.13_spmd, %region_14.16_spmd} | conditional | flops 1102061568 | bytes 48693852 | solution.py:59
  240.1 4.2 %bitcast_add_fusion.1 = f32[128,4,8,128]{3,0,2,1:T(8,128)S(1)} fusion(f32[128,4,8,128]{3,0,2,1:T(8,128)S(1)} %copy-done.2, f32[4,512,128,8]{2,1,3,0:T(8,128)S(1)} %get-tuple-element.654, f32[128,4,8]{0,2,1:T(8,128)S(1)} %max.13, pred[128,512]{0,1:T(8,128)(4,1)S(1)} %get-tuple-element.357, f32[128,4,8]{0,2,1:T(8,128)S(1)} %get-tuple-element.636, ...), kind=kOutput, calls=%fused_computation.30 | convolution fusion | flops 548405248 | bytes 13206016 | tf_op jit(solution)/shard_map/while/body/eval_jaxpr/cond/branch_1_fun/qghk,kgd->qghd/dot_general | solution.py:44
  247.3 9.0 %conditional.10 = ((f32[128,4,8,128]{3,0,2,1:T(8,128)}, f32[128,4,8]{0,2,1:T(8,128)S(1)}, f32[128,4,8]{0,2,1:T(8,128)S(1)})) conditional(s32[]{:T(128)} %convert_element_type.73, (f32[128,4,8,128]{3,0,2,1:T(8,128)}, f32[128,4,8]{0,2,1:T(8,128)S(1)}, f32[128,4,8]{0,2,1:T(8,128)S(1)}) %tuple.130, (pred[128,512]{0,1:T(8,128)(4,1)S(1)}, ...), branch_computations={%region_13.13_spmd, %region_14.16_spmd} | conditional | flops 1102061568 | bytes 48693852 | solution.py:59
  250.8 4.2 %bitcast_add_fusion.1 = f32[128,4,8,128]{3,0,2,1:T(8,128)S(1)} fusion(f32[128,4,8,128]{3,0,2,1:T(8,128)S(1)} %copy-done.2, f32[4,512,128,8]{2,1,3,0:T(8,128)S(1)} %get-tuple-element.654, f32[128,4,8]{0,2,1:T(8,128)S(1)} %max.13, pred[128,512]{0,1:T(8,128)(4,1)S(1)} %get-tuple-element.357, f32[128,4,8]{0,2,1:T(8,128)S(1)} %get-tuple-element.636, ...), kind=kOutput, calls=%fused_computation.30 | convolution fusion | flops 548405248 | bytes 13206016 | tf_op jit(solution)/shard_map/while/body/eval_jaxpr/cond/branch_1_fun/qghk,kgd->qghd/dot_general | solution.py:44
  257.9 9.0 %conditional.10 = ((f32[128,4,8,128]{3,0,2,1:T(8,128)}, f32[128,4,8]{0,2,1:T(8,128)S(1)}, f32[128,4,8]{0,2,1:T(8,128)S(1)})) conditional(s32[]{:T(128)} %convert_element_type.73, (f32[128,4,8,128]{3,0,2,1:T(8,128)}, f32[128,4,8]{0,2,1:T(8,128)S(1)}, f32[128,4,8]{0,2,1:T(8,128)S(1)}) %tuple.130, (pred[128,512]{0,1:T(8,128)(4,1)S(1)}, ...), branch_computations={%region_13.13_spmd, %region_14.16_spmd} | conditional | flops 1102061568 | bytes 48693852 | solution.py:59
  261.4 4.2 %bitcast_add_fusion.1 = f32[128,4,8,128]{3,0,2,1:T(8,128)S(1)} fusion(f32[128,4,8,128]{3,0,2,1:T(8,128)S(1)} %copy-done.2, f32[4,512,128,8]{2,1,3,0:T(8,128)S(1)} %get-tuple-element.654, f32[128,4,8]{0,2,1:T(8,128)S(1)} %max.13, pred[128,512]{0,1:T(8,128)(4,1)S(1)} %get-tuple-element.357, f32[128,4,8]{0,2,1:T(8,128)S(1)} %get-tuple-element.636, ...), kind=kOutput, calls=%fused_computation.30 | convolution fusion | flops 548405248 | bytes 13206016 | tf_op jit(solution)/shard_map/while/body/eval_jaxpr/cond/branch_1_fun/qghk,kgd->qghd/dot_general | solution.py:44
  268.5 8.9 %conditional.10 = ((f32[128,4,8,128]{3,0,2,1:T(8,128)}, f32[128,4,8]{0,2,1:T(8,128)S(1)}, f32[128,4,8]{0,2,1:T(8,128)S(1)})) conditional(s32[]{:T(128)} %convert_element_type.73, (f32[128,4,8,128]{3,0,2,1:T(8,128)}, f32[128,4,8]{0,2,1:T(8,128)S(1)}, f32[128,4,8]{0,2,1:T(8,128)S(1)}) %tuple.130, (pred[128,512]{0,1:T(8,128)(4,1)S(1)}, ...), branch_computations={%region_13.13_spmd, %region_14.16_spmd} | conditional | flops 1102061568 | bytes 48693852 | solution.py:59
  272.0 4.2 %bitcast_add_fusion.1 = f32[128,4,8,128]{3,0,2,1:T(8,128)S(1)} fusion(f32[128,4,8,128]{3,0,2,1:T(8,128)S(1)} %copy-done.2, f32[4,512,128,8]{2,1,3,0:T(8,128)S(1)} %get-tuple-element.654, f32[128,4,8]{0,2,1:T(8,128)S(1)} %max.13, pred[128,512]{0,1:T(8,128)(4,1)S(1)} %get-tuple-element.357, f32[128,4,8]{0,2,1:T(8,128)S(1)} %get-tuple-element.636, ...), kind=kOutput, calls=%fused_computation.30 | convolution fusion | flops 548405248 | bytes 13206016 | tf_op jit(solution)/shard_map/while/body/eval_jaxpr/cond/branch_1_fun/qghk,kgd->qghd/dot_general | solution.py:44
  277.5 43.2 %all-gather.8.cloned.1.call-done = bf16[2048,1024]{1,0:T(8,128)(2,1)} async-done(((bf16[128,1024]{1,0:T(8,128)(2,1)}), bf16[2048,1024]{1,0:T(8,128)(2,1)}) %all-gather.8.cloned.1.call-update) | async-done | bytes 4194320 | tf_op jit(solution)/shard_map/all_gather | solution.py:27
  320.7 3.8 fusion.66
  328.6 4.0 %reshape.93 = bf16[4,512,4,128]{3,2,1,0:T(4,128)(2,1)} reshape(bf16[2048,512]{1,0:T(8,128)(2,1)} %get-tuple-element.657) | data formatting | bytes 4194304 | tf_op jit(solution)/shard_map/reshape | solution.py:71
  336.0 42.5 %while.47 = (s32[]{:T(128)}, f32[128,4,8,128]{3,0,2,1:T(8,128)}, f32[128,4,8]{0,2,1:T(8,128)S(1)}, f32[128,4,8]{0,2,1:T(8,128)S(1)}, s32[4,512]{1,0:T(4,128)S(1)...) while((s32[]{:T(128)}, f32[128,4,8,128]{3,0,2,1:T(8,128)}, ...), condition=%wide.region_25.26_spmd.clone, body=%wide.region_18.25_spmd.clone.sunk | while | flops 1102413952 | bytes 48774520 | solution.py:80
  337.6 8.9 %conditional.11 = ((f32[128,4,8,128]{3,0,2,1:T(8,128)}, f32[128,4,8]{0,2,1:T(8,128)S(1)}, f32[128,4,8]{0,2,1:T(8,128)S(1)})) conditional(s32[]{:T(128)} %convert_element_type.75, (f32[128,4,8,128]{3,0,2,1:T(8,128)}, f32[128,4,8]{0,2,1:T(8,128)S(1)}, f32[128,4,8]{0,2,1:T(8,128)S(1)}) %tuple.135, (pred[128,512]{0,1:T(8,128)(4,1)S(1)}, ...), branch_computations={%region_21.21_spmd, %region_22.24_spmd} | conditional | flops 1102061568 | bytes 48693852 | solution.py:59
  341.1 4.2 %bitcast_add_fusion.2 = f32[128,4,8,128]{3,0,2,1:T(8,128)S(1)} fusion(f32[128,4,8,128]{3,0,2,1:T(8,128)S(1)} %copy-done.4, f32[4,512,128,8]{2,1,3,0:T(8,128)S(1)} %get-tuple-element.656, f32[128,4,8]{0,2,1:T(8,128)S(1)} %max.14, pred[128,512]{0,1:T(8,128)(4,1)S(1)} %get-tuple-element.380, f32[128,4,8]{0,2,1:T(8,128)S(1)} %get-tuple-element.638, ...), kind=kOutput, calls=%fused_computation.50 | convolution fusion | flops 548405248 | bytes 13206016 | tf_op jit(solution)/shard_map/while/body/eval_jaxpr/cond/branch_1_fun/qghk,kgd->qghd/dot_general | solution.py:44
  348.3 9.0 %conditional.11 = ((f32[128,4,8,128]{3,0,2,1:T(8,128)}, f32[128,4,8]{0,2,1:T(8,128)S(1)}, f32[128,4,8]{0,2,1:T(8,128)S(1)})) conditional(s32[]{:T(128)} %convert_element_type.75, (f32[128,4,8,128]{3,0,2,1:T(8,128)}, f32[128,4,8]{0,2,1:T(8,128)S(1)}, f32[128,4,8]{0,2,1:T(8,128)S(1)}) %tuple.135, (pred[128,512]{0,1:T(8,128)(4,1)S(1)}, ...), branch_computations={%region_21.21_spmd, %region_22.24_spmd} | conditional | flops 1102061568 | bytes 48693852 | solution.py:59
  351.7 4.2 %bitcast_add_fusion.2 = f32[128,4,8,128]{3,0,2,1:T(8,128)S(1)} fusion(f32[128,4,8,128]{3,0,2,1:T(8,128)S(1)} %copy-done.4, f32[4,512,128,8]{2,1,3,0:T(8,128)S(1)} %get-tuple-element.656, f32[128,4,8]{0,2,1:T(8,128)S(1)} %max.14, pred[128,512]{0,1:T(8,128)(4,1)S(1)} %get-tuple-element.380, f32[128,4,8]{0,2,1:T(8,128)S(1)} %get-tuple-element.638, ...), kind=kOutput, calls=%fused_computation.50 | convolution fusion | flops 548405248 | bytes 13206016 | tf_op jit(solution)/shard_map/while/body/eval_jaxpr/cond/branch_1_fun/qghk,kgd->qghd/dot_general | solution.py:44
  358.9 9.0 %conditional.11 = ((f32[128,4,8,128]{3,0,2,1:T(8,128)}, f32[128,4,8]{0,2,1:T(8,128)S(1)}, f32[128,4,8]{0,2,1:T(8,128)S(1)})) conditional(s32[]{:T(128)} %convert_element_type.75, (f32[128,4,8,128]{3,0,2,1:T(8,128)}, f32[128,4,8]{0,2,1:T(8,128)S(1)}, f32[128,4,8]{0,2,1:T(8,128)S(1)}) %tuple.135, (pred[128,512]{0,1:T(8,128)(4,1)S(1)}, ...), branch_computations={%region_21.21_spmd, %region_22.24_spmd} | conditional | flops 1102061568 | bytes 48693852 | solution.py:59
  362.4 4.2 %bitcast_add_fusion.2 = f32[128,4,8,128]{3,0,2,1:T(8,128)S(1)} fusion(f32[128,4,8,128]{3,0,2,1:T(8,128)S(1)} %copy-done.4, f32[4,512,128,8]{2,1,3,0:T(8,128)S(1)} %get-tuple-element.656, f32[128,4,8]{0,2,1:T(8,128)S(1)} %max.14, pred[128,512]{0,1:T(8,128)(4,1)S(1)} %get-tuple-element.380, f32[128,4,8]{0,2,1:T(8,128)S(1)} %get-tuple-element.638, ...), kind=kOutput, calls=%fused_computation.50 | convolution fusion | flops 548405248 | bytes 13206016 | tf_op jit(solution)/shard_map/while/body/eval_jaxpr/cond/branch_1_fun/qghk,kgd->qghd/dot_general | solution.py:44
  369.5 9.0 %conditional.11 = ((f32[128,4,8,128]{3,0,2,1:T(8,128)}, f32[128,4,8]{0,2,1:T(8,128)S(1)}, f32[128,4,8]{0,2,1:T(8,128)S(1)})) conditional(s32[]{:T(128)} %convert_element_type.75, (f32[128,4,8,128]{3,0,2,1:T(8,128)}, f32[128,4,8]{0,2,1:T(8,128)S(1)}, f32[128,4,8]{0,2,1:T(8,128)S(1)}) %tuple.135, (pred[128,512]{0,1:T(8,128)(4,1)S(1)}, ...), branch_computations={%region_21.21_spmd, %region_22.24_spmd} | conditional | flops 1102061568 | bytes 48693852 | solution.py:59
  373.0 4.2 %bitcast_add_fusion.2 = f32[128,4,8,128]{3,0,2,1:T(8,128)S(1)} fusion(f32[128,4,8,128]{3,0,2,1:T(8,128)S(1)} %copy-done.4, f32[4,512,128,8]{2,1,3,0:T(8,128)S(1)} %get-tuple-element.656, f32[128,4,8]{0,2,1:T(8,128)S(1)} %max.14, pred[128,512]{0,1:T(8,128)(4,1)S(1)} %get-tuple-element.380, f32[128,4,8]{0,2,1:T(8,128)S(1)} %get-tuple-element.638, ...), kind=kOutput, calls=%fused_computation.50 | convolution fusion | flops 548405248 | bytes 13206016 | tf_op jit(solution)/shard_map/while/body/eval_jaxpr/cond/branch_1_fun/qghk,kgd->qghd/dot_general | solution.py:44
  (172 shorter events, 98.7 us)
Async XLA Ops:
  6.5 107.5 %all-gather.4.cloned.1.call-start = ((), (), s32[]{:S(2)}) async-start(), calls=%async_computation | async-start | bytes 4456448 | tf_op jit(solution)/shard_map/all_gather | solution.py:27
  8.3 211.4 %all-gather.6.cloned.1.call-start = ((), (), s32[]{:S(2)}) async-start(), calls=%async_computation.1 | async-start | bytes 4456448 | tf_op jit(solution)/shard_map/all_gather | solution.py:27
  8.3 6.5 %collective-permute-start = (bf16[128,512]{1,0:T(8,128)(2,1)}, bf16[128,512]{1,0:T(8,128)(2,1)S(1)}, u32[]{:S(2)}, u32[]{:S(2)}) collective-permute-start(bf16[128,512]{1,0:T(8,128)(2,1)} %param.17), channel_id=1, source_target_pairs={{0,16},{16,32},{32,48},{48,64},{64,80},{80,96},{96,112},{112,128},... | collective-permute-start | bytes 393224 | tf_op jit(solution)/shard_map/ppermute | solution.py:18
  10.2 6.5 %collective-permute-start.1 = (bf16[128,512]{1,0:T(8,128)(2,1)}, bf16[128,512]{1,0:T(8,128)(2,1)S(1)}, u32[]{:S(2)}, u32[]{:S(2)}) collective-permute-start(bf16[128,512]{1,0:T(8,128)(2,1)} %param.18), channel_id=1, source_target_pairs={{0,16},{16,32},{32,48},{48,64},{64,80},{80,96},{96,112},{112,128},... | collective-permute-start | bytes 393224 | tf_op jit(solution)/shard_map/ppermute | solution.py:18
  17.5 303.2 %all-gather.8.cloned.1.call-start = ((), (), s32[]{:S(2)}) async-start(), calls=%async_computation.2 | async-start | bytes 4456448 | tf_op jit(solution)/shard_map/all_gather | solution.py:27
  17.5 6.3 %collective-permute-start.2 = (bf16[128,512]{1,0:T(8,128)(2,1)S(1)}, bf16[128,512]{1,0:T(8,128)(2,1)S(1)}, u32[]{:S(2)}, u32[]{:S(2)}) collective-permute-start(bf16[128,512]{1,0:T(8,128)(2,1)S(1)} %collective-permute-done), channel_id=1, source_target_pairs={{0,16},{16,32},{32,48},{48,64},{64,80},{80,96},{96,112},{112,128},... | collective-permute-start | bytes 393224 | tf_op jit(solution)/shard_map/ppermute | solution.py:18
  19.5 6.3 %collective-permute-start.3 = (bf16[128,512]{1,0:T(8,128)(2,1)S(1)}, bf16[128,512]{1,0:T(8,128)(2,1)S(1)}, u32[]{:S(2)}, u32[]{:S(2)}) collective-permute-start(bf16[128,512]{1,0:T(8,128)(2,1)S(1)} %collective-permute-done.1), channel_id=1, source_target_pairs={{0,16},{16,32},{32,48},{48,64},{64,80},{80,96},{96,112},{112,128},... | collective-permute-start | bytes 393224 | tf_op jit(solution)/shard_map/ppermute | solution.py:18
  133.9 2.2 copy-start
  140.3 1.3 copy-start.1
  238.0 2.2 copy-start.2
  244.3 1.3 copy-start.3
  248.6 2.2 copy-start.2
  254.9 1.3 copy-start.3
  259.2 2.2 copy-start.2
  265.6 1.3 copy-start.3
  269.9 2.2 copy-start.2
  276.2 1.3 copy-start.3
  339.0 2.2 copy-start.4
  345.3 1.3 copy-start.5
  349.6 2.2 copy-start.4
  355.9 1.3 copy-start.5
  360.2 2.2 copy-start.4
  366.5 1.3 copy-start.5
  370.8 2.2 copy-start.4
  377.2 1.3 copy-start.5
Sparse Core Ops, SparseCore 0:
  9.1 104.8 all-gather.3
  115.8 103.8 all-gather.5
  221.5 99.1 all-gather.7
where the time goes:
time: 390 us; the launch traced here: 389 us
  waiting for transfers between devices  206 us (53%)
  local copies, waits for them, and re-layouts  64.2 us (16%)
  matrix products  49 us (13%)
  other arithmetic  36.8 us (9%)
  between operations  13.3 us (3%)
  starting transfers between devices  11.1 us (3%)
  loops' own time  8.68 us (2%)
    all_gather x3, waiting for transfers between devices, in_one_piece(): lax.all_gather(both, axis, axis=dim, tiled=True)  200 us
    dot_general x9, matrix products, tile_update(): jnp.einsum('qghk,kgd->qghd', weights.astype(jnp.bfloat16), value_rows, pr...  37.4 us
    unnamed x9, local copies, waits for them, and re-layouts  19.8 us
    reduce_sum x9, other arithmetic, tile_update(): total = total * fade + jnp.sum(weights, axis=3)  19.1 us
    reshape x3, local copies, waits for them, and re-layouts, attend_rows(): value_tiles = value_rows.reshape(count // width, width, GROUPS, HEAD_DIM)  12 us
    cond x45, local copies, waits for them, and re-layouts  11.7 us
    dot_general x9, matrix products, tile_update(): jnp.einsum('qghd,kgd->qghk', query4, key_rows, preferred_element_type=jnp...  11.6 us
    split x3, local copies, waits for them, and re-layouts, in_one_piece(): jnp.split(lax.all_gather(both, axis, axis=dim, tiled=True), ends, axis=al...  11.6 us
  transfers between devices with their start and end apart: 7, of which 7 were waited for; matrix products, arithmetic and copies ran while one was open for 21% of the time, Pallas kernels for 0%

commit v1 on v0

v1 whole, which is shorter than its diff:
```python
import functools
import math

import jax
import jax.numpy as jnp
from jax import lax
from jax.experimental import pallas as pl
from jax.experimental.pallas import tpu as pltpu
from jax.sharding import PartitionSpec as P

HEADS = 32
GROUPS = 4
PER = HEADS // GROUPS
D = 128
TOK = 128
BLOCK = 2048
DOCS = 16
BIG = 2.0**100
SCALE = math.log2(math.e) / math.sqrt(D)
MESH = pl.DeviceIdType.MESH
NT = (((1,), (1,)), ((), ()))
WIDE = 1024
NARROW = 512
ROWS = 256


def kernel(
    lens, q_hbm, k_hbm, v_hbm, out_hbm,
    qin, qa, kv, km, m_ref, acc, obuf,
    s_x, r_x, s_q, r_q, s_z, r_z, s_y, r_y, s_w, r_w, s_c, r_c, s_o, r_o,
):
    o = lax.axis_index("outer")
    i = lax.axis_index("inner")
    x, z = i // 4, i % 4
    c = o % 2

    def at(dx=0, dz=0, do=0):
        return (o + do, ((x + dx) % 4) * 4 + (z + dz) % 4)

    partner = (o + 1 - 2 * c, i)
    has_next = o < 14
    has_prev = o >= 2

    barrier = pltpu.get_barrier_semaphore()
    for d in (1, 2, 3):
        pl.semaphore_signal(barrier, 1, device_id=at(dx=d), device_id_type=MESH)
        pl.semaphore_signal(barrier, 1, device_id=at(dz=d), device_id_type=MESH)
    pl.semaphore_signal(barrier, 1, device_id=partner, device_id_type=MESH)
    pl.semaphore_signal(barrier, 1, device_id=((o + 2) % 16, i), device_id_type=MESH)
    pl.semaphore_signal(barrier, 1, device_id=((o + 14) % 16, i), device_id_type=MESH)
    pl.semaphore_wait(barrier, 9)

    def remote(src, dst, ss, rs, dev):
        return pltpu.make_async_remote_copy(
            src_ref=src, dst_ref=dst, send_sem=ss, recv_sem=rs, device_id=dev, device_id_type=MESH
        )

    def cols(ref, g, width):
        return ref.at[:, pl.ds(pl.multiple_of(g * width, width), width)]

    xs, qs = [], []
    for d in (1, 2, 3):
        g = (x + d) % 4
        xs.append(remote(cols(k_hbm, g, D), kv.at[0, x, z, :, 0:D], s_x.at[d, 0], r_x.at[d, 0], at(dx=d)))
        xs.append(remote(cols(v_hbm, g, D), kv.at[0, x, z, :, D:2 * D], s_x.at[d, 1], r_x.at[d, 1], at(dx=d)))
    for cp in xs:
        cp.start()
    for d in (1, 2, 3):
        g = (x + d) % 4
        qs.append(remote(cols(q_hbm, g, PER * D), qin.at[d], s_q.at[d], r_q.at[d], at(dx=d)))
    for cp in qs:
        cp.start()
    local = [
        pltpu.make_async_copy(cols(k_hbm, x, D), kv.at[0, x, z, :, 0:D], r_x.at[0, 0]),
        pltpu.make_async_copy(cols(v_hbm, x, D), kv.at[0, x, z, :, D:2 * D], r_x.at[0, 1]),
        pltpu.make_async_copy(cols(q_hbm, x, PER * D), qin.at[0], r_q.at[0]),
    ]
    for cp in local:
        cp.start()

    lane = lax.broadcasted_iota(jnp.int32, (1, D), 1)
    start_of = jnp.zeros((1, D), jnp.int32)
    end_of = jnp.zeros((1, D), jnp.int32)
    at_token = jnp.int32(0)
    for n in range(DOCS):
        start_of = jnp.where(lane == n, at_token, start_of)
        at_token = at_token + lens[n]
        end_of = jnp.where(lane == n, at_token, end_of)

    for slot in range(3):
        def mask_rows(t, carry, slot=slot):
            base = pl.multiple_of(t * 256, 256)
            pos = (o - slot) * BLOCK + base + lax.broadcasted_iota(jnp.int32, (256, D), 0)
            here = (pos >= start_of) & (pos < end_of)
            km[slot, pl.ds(base, 256), :] = jnp.where(here, 0.0, -BIG).astype(jnp.bfloat16)
            return carry

        lax.fori_loop(0, BLOCK // 256, mask_rows, 0)

    @pl.when(jnp.logical_not(has_prev))
    def _():
        kv[2] = jnp.zeros(kv.shape[1:], kv.dtype)

    @pl.when(o == 0)
    def _():
        kv[1] = jnp.zeros(kv.shape[1:], kv.dtype)

    for cp in local[:2]:
        cp.wait()
    for cp in xs:
        cp.wait_recv()
    zs = [remote(kv.at[0, :, z], kv.at[0, :, z], s_z.at[d], r_z.at[d], at(dz=d)) for d in (1, 2, 3)]
    for cp in zs:
        cp.start()
    ys = remote(kv.at[0, :, z], kv.at[2, :, z], s_y, r_y, (o + 2, i))

    @pl.when(has_next)
    def _():
        ys.start()

    ws = [remote(kv.at[2, :, z], kv.at[2, :, z], s_w.at[d], r_w.at[d], at(dz=d)) for d in (1, 2, 3)]

    @pl.when(has_prev)
    def _():
        ys.wait_recv()
        for cp in ws:
            cp.start()

    for cp in zs:
        cp.wait_recv()

    give_own = remote(kv.at[0], kv.at[1], s_c, r_c, partner)
    give_old = remote(kv.at[2], kv.at[1], s_c, r_c, partner)

    @pl.when(c == 0)
    def _():
        give_own.start()

    @pl.when(has_prev)
    def _():
        for cp in ws:
            cp.wait_recv()

    @pl.when((c == 1) & has_prev)
    def _():
        give_old.start()

    @pl.when((c == 1) | has_prev)
    def _():
        give_own.wait_recv()

    diag_rows = lax.broadcasted_iota(jnp.int32, (TOK, NARROW), 0)
    diag_cols = lax.broadcasted_iota(jnp.int32, (TOK, NARROW), 1)
    causal = jnp.where(diag_cols <= diag_rows + z * TOK, 0.0, -BIG)
    ones = jnp.where(lax.broadcasted_iota(jnp.int32, (WIDE, D), 1) == 0, 1.0, 0.0).astype(jnp.bfloat16)

    def tile(d, slot, first, size, diag):
        pieces = size // NARROW
        key_value = kv[slot, pl.ds(first // NARROW, pieces)].reshape(size, 2 * D)
        mask = km[slot, pl.ds(pl.multiple_of(first, NARROW), size), :]
        keys = jnp.concatenate([key_value[:, :D], mask], axis=1)
        values = jnp.concatenate([key_value[:, D:], ones[:size]], axis=1)
        for r in range(PER * TOK // ROWS):
            rows = pl.ds(r * ROWS, ROWS)
            s = lax.dot_general(qa[d, rows, :], keys, NT, preferred_element_type=jnp.float32)
            if diag:
                s = s + jnp.concatenate([causal] * (ROWS // TOK), axis=0)
            old = m_ref[rows, :]
            new = jnp.maximum(old, jnp.max(s, axis=1, keepdims=True) * SCALE)
            w = jnp.exp2(s * SCALE - jnp.tile(new, (1, size // D)))
            fade = jnp.exp2(old - new)
            m_ref[rows, :] = new
            mixed = jnp.dot(w.astype(jnp.bfloat16), values, preferred_element_type=jnp.float32)
            acc[rows, :] = acc[rows, :] * jnp.tile(fade, (1, 2)) + mixed

    outs = []
    for d in range(4):
        j = (x - d + 4) % 4
        if d == 0:
            local[2].wait()
        else:
            qs[d - 1].wait_recv()
        qpos = o * BLOCK + (j * 4 + z) * TOK + lax.broadcasted_iota(jnp.int32, (TOK, D), 0)
        mine = jnp.where((qpos >= start_of) & (qpos < end_of), 1.0, 0.0).astype(jnp.bfloat16)
        for h in range(PER):
            qa[d, h * TOK:(h + 1) * TOK, :D] = qin[d, :, h * D:(h + 1) * D]
            qa[d, h * TOK:(h + 1) * TOK, D:] = mine
        m_ref[...] = jnp.full(m_ref.shape, -BIG, jnp.float32)
        acc[...] = jnp.zeros(acc.shape, jnp.float32)
        tile(d, 0, j * NARROW, NARROW, True)

        def near(t, carry, d=d):
            tile(d, 0, t * NARROW, NARROW, False)
            return carry

        lax.fori_loop(0, j, near, 0)

        def far(t, carry, d=d):
            tile(d, 1 + t // (BLOCK // WIDE), (t % (BLOCK // WIDE)) * WIDE, WIDE, False)
            return carry

        lax.fori_loop(0, 2 * BLOCK // WIDE, far, 0)
        for h in range(PER):
            part = acc[h * TOK:(h + 1) * TOK, :]
            obuf[d, :, h * D:(h + 1) * D] = (part[:, :D] / part[:, D:D + 1]).astype(jnp.bfloat16)
        dst = cols(out_hbm, x, PER * D)
        if d == 0:
            cp = pltpu.make_async_copy(obuf.at[0], dst, r_o.at[0])
        else:
            cp = remote(obuf.at[d], dst, s_o.at[d], r_o.at[d], at(dx=4 - d))
        cp.start()
        outs.append(cp)

    for cp in outs:
        cp.wait()
    for cp in xs + qs:
        cp.wait_send()
    for cp in zs:
        cp.wait_send()

    @pl.when(has_next)
    def _():
        ys.wait_send()

    @pl.when(has_prev)
    def _():
        for cp in ws:
            cp.wait_send()

    @pl.when((c == 0) | has_prev)
    def _():
        give_own.wait_send()


def body(queries, keys, values, doc_lengths):
    any_ref = pl.BlockSpec(memory_space=pl.ANY)
    dma = pltpu.SemaphoreType.DMA
    bf16, f32 = jnp.bfloat16, jnp.float32
    return pl.pallas_call(
        kernel,
        out_shape=jax.ShapeDtypeStruct(queries.shape, bf16),
        in_specs=[pl.BlockSpec(memory_space=pltpu.SMEM), any_ref, any_ref, any_ref],
        out_specs=any_ref,
        scratch_shapes=[
            pltpu.VMEM((4, TOK, PER * D), bf16),
            pltpu.VMEM((4, PER * TOK, 2 * D), bf16),
            pltpu.VMEM((3, 4, 4, TOK, 2 * D), bf16),
            pltpu.VMEM((3, BLOCK, D), bf16),
            pltpu.VMEM((PER * TOK, D), f32),
            pltpu.VMEM((PER * TOK, 2 * D), f32),
            pltpu.VMEM((4, TOK, PER * D), bf16),
            dma((4, 2)), dma((4, 2)), dma((4,)), dma((4,)), dma((4,)), dma((4,)), dma, dma,
            dma((4,)), dma((4,)), dma, dma, dma((4,)), dma((4,)),
        ],
        compiler_params=pltpu.CompilerParams(
            collective_id=0, has_side_effects=True, vmem_limit_bytes=48 << 20
        ),
        cost_estimate=pl.CostEstimate(flops=13 * 10**9, bytes_accessed=4 << 20, transcendentals=22 * 10**6),
        name="attend",
    )(doc_lengths, queries, keys, values)


def solution(mesh):
    rows = P(("outer", "inner"), None)
    return jax.shard_map(
        body, mesh=mesh, in_specs=(rows, rows, rows, P()), out_specs=rows, check_vma=False
    )
```

time: 390 us -> 117 us (0.30)
  the two profiles are of different devices: /device:TPU:8 before, /device:TPU:224 now
where the time goes in v1:
time: 117 us; the launch traced here: 116 us
  Pallas kernels  111 us (95%)
  local copies, waits for them, and re-layouts  4.66 us (4%)
    pallas_call x1, Pallas kernels, body(): pl.pallas_call(kernel, out_shape=jax.ShapeDtypeStruct(queries.shape, bf16...  111 us
    unnamed x9, local copies, waits for them, and re-layouts  4.66 us

profile of v1, /device:TPU:224, one launch (start us, length us, event | category | flops | bytes accessed | tf_op | source)
XLA Modules:
  0.0 116.1 jit_solution(7163054646071235418)
XLA Ops:
  0.0 0.0 copy-start
  0.0 1.2 %copy-done = bf16[128,4096]{1,0:T(8,128)(2,1)S(1)} copy-done((bf16[128,4096]{1,0:T(8,128)(2,1)S(1)}, bf16[128,4096]{1,0:T(8,128)(2,1)}, u32[]{:S(2)}) %copy-start) | copy-done | bytes 1048600
  1.2 0.0 copy-start.1
  1.2 0.9 copy-done.1
  2.1 0.0 copy-start.2
  2.1 0.9 copy-done.2
  3.0 0.0 copy-start.3
  3.0 0.7 copy-done.3
  3.7 111.4 %attend.1 = bf16[128,4096]{1,0:T(8,128)(2,1)S(1)} custom-call(s32[16]{0:T(128)S(1)} %copy-done.3, bf16[128,4096]{1,0:T(8,128)(2,1)S(1)} %copy-done, bf16[128,512]{1,0:T(8,128)(2,1)S(1)} %copy-done.1, bf16[128,512]{1,0:T(8,128)(2,1)S(1)} %copy-done.2), custom_call_target="tpu_custom_call" | custom-call | flops 12999999488 | bytes 4194304 | tf_op jit(solution)/shard_map/attend/pallas_call | solution.py:239
  115.1 1.0 copy.6
Async XLA Ops:
  0.0 1.2 %copy-start = (bf16[128,4096]{1,0:T(8,128)(2,1)S(1)}, bf16[128,4096]{1,0:T(8,128)(2,1)}, u32[]{:S(2)}) copy-start(bf16[128,4096]{1,0:T(8,128)(2,1)} %q_hbm.1) | copy-start | bytes 3145732
  1.2 0.9 copy-start.1
  2.1 0.9 copy-start.2
  3.0 0.7 copy-start.3

commit v2 on v1

v2 whole, which is shorter than its diff:
```python
import functools
import math

import jax
import jax.numpy as jnp
from jax import lax
from jax.experimental import pallas as pl
from jax.experimental.pallas import tpu as pltpu
from jax.sharding import PartitionSpec as P

HEADS = 32
GROUPS = 4
PER = HEADS // GROUPS
D = 128
TOK = 128
BLOCK = 2048
DOCS = 16
BIG = 2.0**100
SCALE = math.log2(math.e) / math.sqrt(D)
MESH = pl.DeviceIdType.MESH
NT = (((1,), (1,)), ((), ()))
WIDE = 1024
NARROW = 512
ROWS = 256


def kernel(
    lens, q_hbm, k_hbm, v_hbm, out_hbm,
    qin, qa, kv, km, m_ref, acc, obuf,
    s_x, r_x, s_q, r_q, s_z, r_z, s_y, r_y, s_h, r_h, s_w, r_w, s_c, r_c, s_o, r_o,
):
    o = lax.axis_index("outer")
    i = lax.axis_index("inner")
    x, z = i // 4, i % 4
    c = o % 2

    def at(dx=0, dz=0, do=0):
        return (o + do, ((x + dx) % 4) * 4 + (z + dz) % 4)

    partner = (o + 1 - 2 * c, i)
    has_prev = o >= 2
    send_far = (o % 8 >= 6) & (o < 14)
    send_near = o % 8 < 6
    from_far = (o % 8 < 2) & has_prev
    from_near = o % 8 >= 2

    barrier = pltpu.get_barrier_semaphore()
    for d in (1, 2, 3):
        pl.semaphore_signal(barrier, 1, device_id=at(dx=d), device_id_type=MESH)
        pl.semaphore_signal(barrier, 1, device_id=at(dz=d), device_id_type=MESH)
    pl.semaphore_signal(barrier, 1, device_id=partner, device_id_type=MESH)
    pl.semaphore_signal(barrier, 1, device_id=((o + 2) % 16, i), device_id_type=MESH)
    pl.semaphore_signal(barrier, 1, device_id=((o + 14) % 16, i), device_id_type=MESH)
    pl.semaphore_wait(barrier, 9)

    def remote(src, dst, ss, rs, dev):
        return pltpu.make_async_remote_copy(
            src_ref=src, dst_ref=dst, send_sem=ss, recv_sem=rs, device_id=dev, device_id_type=MESH
        )

    def arrived(ref, sem):
        pltpu.make_async_copy(ref, ref, sem).wait()

    def cols(ref, g, width):
        return ref.at[:, pl.ds(pl.multiple_of(g * width, width), width)]

    xs, qs = [], []
    for d in (1, 2, 3):
        g = (x + d) % 4
        xs.append(remote(cols(k_hbm, g, D), kv.at[0, x, z, :, 0:D], s_x.at[d, 0], r_x.at[x], at(dx=d)))
        xs.append(remote(cols(v_hbm, g, D), kv.at[0, x, z, :, D:2 * D], s_x.at[d, 1], r_x.at[x], at(dx=d)))
    local = [
        pltpu.make_async_copy(cols(k_hbm, x, D), kv.at[0, x, z, :, 0:D], r_x.at[x]),
        pltpu.make_async_copy(cols(v_hbm, x, D), kv.at[0, x, z, :, D:2 * D], r_x.at[x]),
        pltpu.make_async_copy(cols(q_hbm, x, PER * D), qin.at[0], r_q.at[0]),
    ]
    for cp in xs + local:
        cp.start()
    for d in (1, 2, 3):
        g = (x + d) % 4
        qs.append(remote(cols(q_hbm, g, PER * D), qin.at[d], s_q.at[d], r_q.at[d], at(dx=d)))
    for cp in qs:
        cp.start()

    lane = lax.broadcasted_iota(jnp.int32, (1, D), 1)
    start_of = jnp.zeros((1, D), jnp.int32)
    end_of = jnp.zeros((1, D), jnp.int32)
    at_token = jnp.int32(0)
    for n in range(DOCS):
        start_of = jnp.where(lane == n, at_token, start_of)
        at_token = at_token + lens[n]
        end_of = jnp.where(lane == n, at_token, end_of)

    def mask_rows(t, carry):
        base = pl.multiple_of((t % 8) * 256, 256)
        pos = (o - t // 8) * BLOCK + base + lax.broadcasted_iota(jnp.int32, (256, D), 0)
        here = (pos >= start_of) & (pos < end_of)
        km[t // 8, pl.ds(base, 256), :] = jnp.where(here, 0.0, -BIG).astype(jnp.bfloat16)
        return carry

    lax.fori_loop(0, 3 * BLOCK // 256, mask_rows, 0)
    m_ref[...] = jnp.full(m_ref.shape, -BIG, jnp.float32)
    acc[...] = jnp.zeros(acc.shape, jnp.float32)

    @pl.when(jnp.logical_not(has_prev))
    def _():
        kv[2] = jnp.zeros(kv.shape[1:], kv.dtype)

    @pl.when(o == 0)
    def _():
        kv[1] = jnp.zeros(kv.shape[1:], kv.dtype)

    zs, hs = [], []
    for p in range(4):
        arrived(kv.at[0, p, z], r_x.at[p])
        for d in (1, 2, 3):
            cp = remote(kv.at[0, p, z], kv.at[0, p, z], s_z.at[d, p], r_z.at[d, p], at(dz=d))
            cp.start()
            zs.append(cp)
        hs.append(remote(kv.at[0, p, z], kv.at[2, p, z], s_h.at[p], r_h.at[p], (o + 2, i)))

    @pl.when(send_far)
    def _():
        for cp in hs:
            cp.start()

    def on_y(p):
        return remote(kv.at[0, p], kv.at[2, p], s_y.at[p], r_y.at[p], (o + 2, i))

    def on_w(p, d):
        return remote(kv.at[2, p, z], kv.at[2, p, z], s_w.at[d, p], r_w.at[d, p], at(dz=d))

    def give(p, slot):
        return remote(kv.at[slot, p], kv.at[1, p], s_c.at[p], r_c.at[p], partner)

    def wait_old(p):
        @pl.when(from_near)
        def _():
            arrived(kv.at[2, p], r_y.at[p])

        @pl.when(from_far)
        def _():
            for d in (1, 2, 3):
                arrived(kv.at[2, p, z], r_w.at[d, p])

    ones = jnp.where(lax.broadcasted_iota(jnp.int32, (WIDE, D), 1) == 0, 1.0, 0.0).astype(jnp.bfloat16)

    def tile(d, slot, first, size, bias=None):
        key_value = kv[slot, pl.ds(first // NARROW, size // NARROW)].reshape(size, 2 * D)
        mask = km[slot, pl.ds(pl.multiple_of(first, NARROW), size), :]
        keys = jnp.concatenate([key_value[:, :D], mask], axis=1)
        values = jnp.concatenate([key_value[:, D:], ones[:size]], axis=1)
        for r in range(PER * TOK // ROWS):
            rows = pl.ds(r * ROWS, ROWS)
            s = lax.dot_general(qa[d, rows, :], keys, NT, preferred_element_type=jnp.float32)
            if bias is not None:
                s = s + jnp.concatenate([bias] * (ROWS // TOK), axis=0)
            old = m_ref[d, rows, :]
            new = jnp.maximum(old, jnp.max(s, axis=1, keepdims=True) * SCALE)
            w = jnp.exp2(s * SCALE - jnp.tile(new, (1, size // D)))
            fade = jnp.exp2(old - new)
            m_ref[d, rows, :] = new
            mixed = jnp.dot(w.astype(jnp.bfloat16), values, preferred_element_type=jnp.float32)
            acc[d, rows, :] = acc[d, rows, :] * jnp.tile(fade, (1, 2)) + mixed

    ahead = lax.broadcasted_iota(jnp.int32, (TOK, NARROW), 1) - lax.broadcasted_iota(
        jnp.int32, (TOK, NARROW), 0
    )

    def own_piece(p, carry):
        for d in (1, 2, 3):
            arrived(kv.at[0, p, z], r_z.at[d, p])

        @pl.when(send_near)
        def _():
            on_y(p).start()

        @pl.when(c == 0)
        def _():
            give(p, 0).start()

        def own_chunk(d, carry):
            j = (x - d + 4) % 4

            @pl.when(p == 0)
            def _():
                arrived(qin.at[d], r_q.at[d])
                qpos = o * BLOCK + (j * 4 + z) * TOK + lax.broadcasted_iota(jnp.int32, (TOK, D), 0)
                mine = jnp.where((qpos >= start_of) & (qpos < end_of), 1.0, 0.0).astype(jnp.bfloat16)
                for h in range(PER):
                    qa[d, h * TOK:(h + 1) * TOK, :D] = qin[d, :, h * D:(h + 1) * D]
                    qa[d, h * TOK:(h + 1) * TOK, D:] = mine

            @pl.when(j >= p)
            def _():
                bias = jnp.where(ahead <= (j - p) * NARROW + z * TOK, 0.0, -BIG)
                tile(d, 0, p * NARROW, NARROW, bias)

            return carry

        lax.fori_loop(0, 4, own_chunk, 0)

        @pl.when(from_far)
        def _():
            arrived(kv.at[2, p, z], r_h.at[p])
            for d in (1, 2, 3):
                on_w(p, d).start()

        return carry

    lax.fori_loop(0, 4, own_piece, 0)

    def first_earlier(t, carry):
        for p in (2 * t, 2 * t + 1):
            @pl.when(c == 0)
            def _():
                wait_old(p)

            @pl.when(c == 1)
            def _():
                arrived(kv.at[1, p], r_c.at[p])

        def chunk(d, carry):
            tile(d, 2 - c, t * WIDE, WIDE)

            @pl.when((c == 1) & has_prev & (t == 0))
            def _():
                wait_old(d)
                give(d, 2).start()

            return carry

        return lax.fori_loop(0, 4, chunk, carry)

    lax.fori_loop(0, BLOCK // WIDE, first_earlier, 0)

    @pl.when((c == 0) & has_prev)
    def _():
        for p in range(4):
            arrived(kv.at[1, p], r_c.at[p])

    def send_out(d):
        return remote(obuf.at[d], cols(out_hbm, x, PER * D), s_o.at[d], r_o.at[d], at(dx=4 - d))

    keep = pltpu.make_async_copy(obuf.at[0], cols(out_hbm, x, PER * D), r_o.at[0])

    def last_earlier(n, carry):
        d = (n + 1) % 4

        def far(t, carry):
            tile(d, 1 + c, t * WIDE, WIDE)
            return carry

        lax.fori_loop(0, BLOCK // WIDE, far, 0)
        for h in range(PER):
            part = acc[d, h * TOK:(h + 1) * TOK, :]
            obuf[d, :, h * D:(h + 1) * D] = (part[:, :D] / part[:, D:D + 1]).astype(jnp.bfloat16)

        @pl.when(d > 0)
        def _():
            send_out(d).start()

        @pl.when(d == 0)
        def _():
            keep.start()

        return carry

    lax.fori_loop(0, 4, last_earlier, 0)

    keep.wait()
    for d in (1, 2, 3):
        send_out(d).wait()
    for cp in xs + qs + zs:
        cp.wait_send()

    @pl.when(send_near)
    def _():
        for p in range(4):
            on_y(p).wait_send()

    @pl.when(send_far)
    def _():
        for cp in hs:
            cp.wait_send()

    @pl.when(from_far)
    def _():
        for p in range(4):
            for d in (1, 2, 3):
                on_w(p, d).wait_send()

    @pl.when((c == 0) | has_prev)
    def _():
        for p in range(4):
            give(p, 0).wait_send()


def body(queries, keys, values, doc_lengths):
    any_ref = pl.BlockSpec(memory_space=pl.ANY)
    dma = pltpu.SemaphoreType.DMA
    bf16, f32 = jnp.bfloat16, jnp.float32
    return pl.pallas_call(
        kernel,
        out_shape=jax.ShapeDtypeStruct(queries.shape, bf16),
        in_specs=[pl.BlockSpec(memory_space=pltpu.SMEM), any_ref, any_ref, any_ref],
        out_specs=any_ref,
        scratch_shapes=[
            pltpu.VMEM((4, TOK, PER * D), bf16),
            pltpu.VMEM((4, PER * TOK, 2 * D), bf16),
            pltpu.VMEM((3, 4, 4, TOK, 2 * D), bf16),
            pltpu.VMEM((3, BLOCK, D), bf16),
            pltpu.VMEM((4, PER * TOK, D), f32),
            pltpu.VMEM((4, PER * TOK, 2 * D), f32),
            pltpu.VMEM((4, TOK, PER * D), bf16),
            dma((4, 2)), dma((4,)), dma((4,)), dma((4,)), dma((4, 4)), dma((4, 4)), dma((4,)), dma((4,)),
            dma((4,)), dma((4,)), dma((4, 4)), dma((4, 4)), dma((4,)), dma((4,)), dma((4,)), dma((4,)),
        ],
        compiler_params=pltpu.CompilerParams(
            collective_id=0, has_side_effects=True, vmem_limit_bytes=60 << 20
        ),
        cost_estimate=pl.CostEstimate(flops=13 * 10**9, bytes_accessed=4 << 20, transcendentals=22 * 10**6),
        name="attend",
    )(doc_lengths, queries, keys, values)


def solution(mesh):
    rows = P(("outer", "inner"), None)
    return jax.shard_map(
        body, mesh=mesh, in_specs=(rows, rows, rows, P()), out_specs=rows, check_vma=False
    )
```

time: 117 us -> 89 us (0.76)
  Pallas kernels: 111 us -> 86.6 us
  local copies, waits for them, and re-layouts: 4.66 us -> 2.29 us
    pallas_call x1, Pallas kernels: 111 us -> 86.6 us  [body(): pl.pallas_call(kernel, out_shape=jax.ShapeDtypeStruct(queries.shape, bf16...]
    unnamed x9 -> x1, local copies, waits for them, and re-layouts: 4.66 us -> 2.29 us
where the time goes in v2:
time: 89 us; the launch traced here: 88.9 us
  Pallas kernels  86.6 us (97%)
  local copies, waits for them, and re-layouts  2.29 us (3%)
    pallas_call x1, Pallas kernels, body(): pl.pallas_call(kernel, out_shape=jax.ShapeDtypeStruct(queries.shape, bf16...  86.6 us
    unnamed x1, local copies, waits for them, and re-layouts  2.29 us

profile of v2, /device:TPU:224, one launch (start us, length us, event | category | flops | bytes accessed | tf_op | source)
XLA Modules:
  0.0 88.9 jit_solution(8266909033317103345)
XLA Ops:
  0.0 86.6 %attend.1 = bf16[128,4096]{1,0:T(8,128)(2,1)} custom-call(s32[16]{0:T(128)} %lens.1, bf16[128,4096]{1,0:T(8,128)(2,1)} %q_hbm.1, bf16[128,512]{1,0:T(8,128)(2,1)} %k_hbm.1, bf16[128,512]{1,0:T(8,128)(2,1)} %v_hbm.1), custom_call_target="tpu_custom_call" | custom-call | flops 12999999488 | bytes 4194304 | tf_op jit(solution)/shard_map/attend/pallas_call | solution.py:303
  86.6 2.3 %copy.6 = bf16[128,4096]{1,0:T(8,128)(2,1)} copy(bf16[128,4096]{1,0:T(8,128)(2,1)} %attend.1) | data formatting | bytes 2097152

commit v3 on v2

v3 whole, which is shorter than its diff:
```python
import functools
import math

import jax
import jax.numpy as jnp
from jax import lax
from jax.experimental import pallas as pl
from jax.experimental.pallas import tpu as pltpu
from jax.sharding import PartitionSpec as P

HEADS = 32
GROUPS = 4
PER = HEADS // GROUPS
D = 128
TOK = 128
BLOCK = 2048
DOCS = 16
BIG = 2.0**100
SCALE = math.log2(math.e) / math.sqrt(D)
MESH = pl.DeviceIdType.MESH
NT = (((1,), (1,)), ((), ()))
WIDE = 1024
NARROW = 512
ROWS = 512
CHUNK = PER * TOK


def kernel(
    lens, q_hbm, k_hbm, v_hbm, out_hbm,
    qin, qa, kv, km, m_ref, acc, obuf, held, ready,
    s_x, r_x, s_q, r_q, s_z, r_z, s_y, r_y, s_h, r_h, s_w, r_w, s_c, r_c, s_o, r_o,
):
    o = lax.axis_index("outer")
    i = lax.axis_index("inner")
    x, z = i // 4, i % 4
    c = o % 2

    def at(dx=0, dz=0):
        return (o, ((x + dx) % 4) * 4 + (z + dz) % 4)

    partner = (o + 1 - 2 * c, i)
    has_prev = o >= 2
    has_next = o < 14
    send_far = (o % 8 >= 6) & has_next
    send_near = o % 8 < 6
    from_far = (o % 8 < 2) & has_prev
    from_near = o % 8 >= 2
    relay = o >= 14
    mirror = x * 4 + 3 - z
    mz = 3 - z

    barrier = pltpu.get_barrier_semaphore()
    for d in (1, 2, 3):
        pl.semaphore_signal(barrier, 1, device_id=at(dx=d), device_id_type=MESH)
        pl.semaphore_signal(barrier, 1, device_id=at(dz=d), device_id_type=MESH)
    pl.semaphore_signal(barrier, 1, device_id=partner, device_id_type=MESH)

    @pl.when(has_next)
    def _():
        pl.semaphore_signal(
            barrier, 1, device_id=(o + 2, jnp.where(send_far, mirror, i)), device_id_type=MESH
        )

    @pl.when(send_far)
    def _():
        pl.semaphore_signal(barrier, 1, device_id=(o + 8, mirror), device_id_type=MESH)

    @pl.when(from_far)
    def _():
        for n in range(4):
            pl.semaphore_signal(barrier, 1, device_id=(o + 6, x * 4 + n), device_id_type=MESH)

    pl.semaphore_wait(barrier, 7 + jnp.where(has_prev, 1, 0) + jnp.where(relay, 5, 0))

    @pl.when(has_prev)
    def _():
        pl.semaphore_signal(
            ready, 1, device_id=(o - 2, jnp.where(from_far, mirror, i)), device_id_type=MESH
        )

    @pl.when(relay)
    def _():
        pl.semaphore_signal(ready, 1, device_id=(o - 8, mirror), device_id_type=MESH)

    def remote(src, dst, ss, rs, dev):
        return pltpu.make_async_remote_copy(
            src_ref=src, dst_ref=dst, send_sem=ss, recv_sem=rs, device_id=dev, device_id_type=MESH
        )

    def arrived(ref, sem):
        pltpu.make_async_copy(ref, ref, sem).wait()

    def cols(ref, g, width):
        return ref.at[:, pl.ds(pl.multiple_of(g * width, width), width)]

    xs, qs = [], []
    for d in (1, 2, 3):
        g = (x + d) % 4
        xs.append(remote(cols(k_hbm, g, D), kv.at[0, x, z, :, 0:D], s_x.at[d, 0], r_x.at[x], at(dx=d)))
        xs.append(remote(cols(v_hbm, g, D), kv.at[0, x, z, :, D:2 * D], s_x.at[d, 1], r_x.at[x], at(dx=d)))
    local = [
        pltpu.make_async_copy(cols(k_hbm, x, D), kv.at[0, x, z, :, 0:D], r_x.at[x]),
        pltpu.make_async_copy(cols(v_hbm, x, D), kv.at[0, x, z, :, D:2 * D], r_x.at[x]),
        pltpu.make_async_copy(cols(q_hbm, x, PER * D), qin.at[x], r_q.at[x]),
    ]
    for cp in xs + local:
        cp.start()
    for d in (1, 3, 2):
        g = (x + d) % 4
        qs.append(remote(cols(q_hbm, g, PER * D), qin.at[x], s_q.at[d], r_q.at[x], at(dx=d)))
    for cp in qs:
        cp.start()

    lane = lax.broadcasted_iota(jnp.int32, (1, D), 1)
    start_of = jnp.zeros((1, D), jnp.int32)
    end_of = jnp.zeros((1, D), jnp.int32)
    at_token = jnp.int32(0)
    for n in range(DOCS):
        start_of = jnp.where(lane == n, at_token, start_of)
        at_token = at_token + lens[n]
        end_of = jnp.where(lane == n, at_token, end_of)

    def mask_rows(t, carry):
        base = pl.multiple_of((t % 8) * 256, 256)
        pos = (o - t // 8) * BLOCK + base + lax.broadcasted_iota(jnp.int32, (256, D), 0)
        here = (pos >= start_of) & (pos < end_of)
        km[t // 8, pl.ds(base, 256), :] = jnp.where(here, 0.0, -BIG).astype(jnp.bfloat16)
        return carry

    lax.fori_loop(0, 3 * BLOCK // 256, mask_rows, 0)
    m_ref[...] = jnp.full(m_ref.shape, -BIG, jnp.float32)
    acc[...] = jnp.zeros(acc.shape, jnp.float32)

    @pl.when(jnp.logical_not(has_prev))
    def _():
        kv[2] = jnp.zeros(kv.shape[1:], kv.dtype)

    @pl.when(o == 0)
    def _():
        kv[1] = jnp.zeros(kv.shape[1:], kv.dtype)

    zs, hs = [], []
    for p in range(4):
        arrived(kv.at[0, p, z], r_x.at[p])
        if p == 0:
            @pl.when(has_next)
            def _():
                pl.semaphore_wait(ready, 1 + jnp.where(send_far, 1, 0))

        if p < 2:
            far = remote(kv.at[0, p, z], kv.at[2, p, z], s_h.at[p], r_h.at[p], (o + 2, mirror))
        else:
            far = remote(kv.at[0, p, z], held.at[p - 2], s_h.at[p], r_h.at[p], (o + 8, mirror))
        hs.append(far)

        @pl.when(send_far)
        def _():
            far.start()

        for d in (1, 2, 3):
            cp = remote(kv.at[0, p, z], kv.at[0, p, z], s_z.at[d, p], r_z.at[d, p], at(dz=d))
            cp.start()
            zs.append(cp)

    def on_y(p):
        return remote(kv.at[0, p], kv.at[2, p], s_y.at[p], r_y.at[p], (o + 2, i))

    def on_w(p, d):
        if p < 2:
            return remote(kv.at[2, p, mz], kv.at[2, p, mz], s_w.at[d, p], r_w.at[d, p], at(dz=d))
        to = (o - 6, x * 4 + (z + d) % 4)
        return remote(held.at[p - 2], kv.at[2, p, mz], s_w.at[d, p], r_w.at[d, p], to)

    def give(p, slot):
        return remote(kv.at[slot, p], kv.at[1, p], s_c.at[p], r_c.at[p], partner)

    def wait_old(p):
        @pl.when(from_near)
        def _():
            arrived(kv.at[2, p], r_y.at[p])

        @pl.when(from_far)
        def _():
            for d in (1, 2, 3) if p < 2 else (0, 1, 2, 3):
                arrived(kv.at[2, p, mz], r_w.at[d, p])

    ones = jnp.where(lax.broadcasted_iota(jnp.int32, (WIDE, D), 1) == 0, 1.0, 0.0).astype(jnp.bfloat16)

    def keys_of(slot, first, size):
        key_value = kv[slot, first // NARROW:(first + size) // NARROW].reshape(size, 2 * D)
        mask = km[slot, first:first + size, :]
        keys = jnp.concatenate([key_value[:, :D], mask], axis=1)
        values = jnp.concatenate([key_value[:, D:], ones[:size]], axis=1)
        return keys, values

    def steps(todo):
        def scores(n):
            rows, keys, values, bias = todo[n]
            s = lax.dot_general(qa[rows, :], keys, NT, preferred_element_type=jnp.float32)
            return s if bias is None else s + jnp.concatenate([bias] * (ROWS // TOK), axis=0)

        s = scores(0)
        for n in range(len(todo)):
            later = scores(n + 1) if n + 1 < len(todo) else None
            rows, keys, values, bias = todo[n]
            old = m_ref[rows, :]
            new = jnp.maximum(old, jnp.max(s, axis=1, keepdims=True) * SCALE)
            w = jnp.exp2(s * SCALE - jnp.tile(new, (1, s.shape[1] // D)))
            fade = jnp.exp2(old - new)
            m_ref[rows, :] = new
            mixed = jnp.dot(w.astype(jnp.bfloat16), values, preferred_element_type=jnp.float32)
            acc[rows, :] = acc[rows, :] * jnp.tile(fade, (1, 2)) + mixed
            s = later

    ahead = lax.broadcasted_iota(jnp.int32, (TOK, NARROW), 1) - lax.broadcasted_iota(
        jnp.int32, (TOK, NARROW), 0
    )
    causal = jnp.where(ahead <= z * TOK, 0.0, -BIG)

    def queries_in(d, carry):
        j = (x - d + 4) % 4
        arrived(qin.at[j], r_q.at[j])
        qpos = o * BLOCK + (j * 4 + z) * TOK + lax.broadcasted_iota(jnp.int32, (TOK, D), 0)
        mine = jnp.where((qpos >= start_of) & (qpos < end_of), 1.0, 0.0).astype(jnp.bfloat16)
        for h in range(PER):
            rows = pl.ds(pl.multiple_of(j * CHUNK + h * TOK, TOK), TOK)
            qa[rows, :D] = qin[j, :, h * D:(h + 1) * D]
            qa[rows, D:] = mine
        return carry

    def own(p):
        for d in (1, 2, 3):
            arrived(kv.at[0, p, z], r_z.at[d, p])

        @pl.when(send_near)
        def _():
            on_y(p).start()

        @pl.when(c == 0)
        def _():
            give(p, 0).start()

        if p == 0:
            lax.fori_loop(0, 4, queries_in, 0)
        if p == 3:
            @pl.when(from_far)
            def _():
                for n in (0, 1):
                    arrived(kv.at[2, n, mz], r_h.at[n])
                    for d in (1, 2, 3):
                        on_w(n, d).start()

            @pl.when(relay)
            def _():
                for n in (2, 3):
                    arrived(held.at[n - 2], r_h.at[n])
                    for d in (0, 1, 2, 3):
                        on_w(n, d).start()

        keys, values = keys_of(0, p * NARROW, NARROW)
        todo = []
        for r in range(p * CHUNK, 4 * CHUNK, ROWS):
            todo.append((slice(r, r + ROWS), keys, values, causal if r < (p + 1) * CHUNK else None))
        steps(todo)

    def earlier(p):
        @pl.when(c == 0)
        def _():
            wait_old(p)

        @pl.when(c == 1)
        def _():
            arrived(kv.at[1, p], r_c.at[p])

        @pl.when((c == 1) & has_prev)
        def _():
            for n in {0: (), 1: (0,), 2: (1,), 3: (2, 3)}[p]:
                wait_old(n)
                give(n, 2).start()

        keys, values = keys_of(2 - c, p * NARROW, NARROW)
        steps([(slice(r, r + ROWS), keys, values, None) for r in range(0, 4 * CHUNK, ROWS)])

    for p in range(4):
        own(p)
    for p in range(4):
        earlier(p)

    @pl.when((c == 0) & has_prev)
    def _():
        for p in range(4):
            arrived(kv.at[1, p], r_c.at[p])

    def send_out(d):
        return remote(obuf.at[d], cols(out_hbm, x, PER * D), s_o.at[d], r_o.at[d], at(dx=d))

    keep = pltpu.make_async_copy(obuf.at[0], cols(out_hbm, x, PER * D), r_o.at[0])

    def last(n, carry):
        d = jnp.where(n == 0, 2, jnp.where(n == 1, 1, jnp.where(n == 2, 3, 0)))
        base = ((x + d) % 4) * CHUNK
        todo = []
        for first in range(0, BLOCK, WIDE):
            keys, values = keys_of(1 + c, first, WIDE)
            for r in range(0, CHUNK, ROWS):
                todo.append((pl.ds(pl.multiple_of(base + r, ROWS), ROWS), keys, values, None))
        steps(todo)
        for h in range(PER):
            part = acc[pl.ds(pl.multiple_of(base + h * TOK, TOK), TOK), :]
            obuf[d, :, h * D:(h + 1) * D] = (part[:, :D] / part[:, D:D + 1]).astype(jnp.bfloat16)

        @pl.when(d > 0)
        def _():
            send_out(d).start()

        @pl.when(d == 0)
        def _():
            keep.start()

        return carry

    lax.fori_loop(0, 4, last, 0)

    keep.wait()
    for d in (1, 2, 3):
        send_out(d).wait()
    for cp in xs + qs + zs:
        cp.wait_send()

    @pl.when(send_near)
    def _():
        for p in range(4):
            on_y(p).wait_send()

    @pl.when(send_far)
    def _():
        for cp in hs:
            cp.wait_send()

    @pl.when(from_far)
    def _():
        for p in (0, 1):
            for d in (1, 2, 3):
                on_w(p, d).wait_send()

    @pl.when(relay)
    def _():
        for p in (2, 3):
            for d in (0, 1, 2, 3):
                on_w(p, d).wait_send()

    @pl.when((c == 0) | has_prev)
    def _():
        for p in range(4):
            give(p, 0).wait_send()


def body(queries, keys, values, doc_lengths):
    hbm = pl.BlockSpec(memory_space=pltpu.HBM)
    dma = pltpu.SemaphoreType.DMA
    bf16, f32 = jnp.bfloat16, jnp.float32
    return pl.pallas_call(
        kernel,
        out_shape=jax.ShapeDtypeStruct(queries.shape, bf16),
        in_specs=[pl.BlockSpec(memory_space=pltpu.SMEM), hbm, hbm, hbm],
        out_specs=pl.BlockSpec(memory_space=pltpu.VMEM),
        scratch_shapes=[
            pltpu.VMEM((4, TOK, PER * D), bf16),
            pltpu.VMEM((4 * CHUNK, 2 * D), bf16),
            pltpu.VMEM((3, 4, 4, TOK, 2 * D), bf16),
            pltpu.VMEM((3, BLOCK, D), bf16),
            pltpu.VMEM((4 * CHUNK, D), f32),
            pltpu.VMEM((4 * CHUNK, 2 * D), f32),
            pltpu.VMEM((4, TOK, PER * D), bf16),
            pltpu.VMEM((2, TOK, 2 * D), bf16),
            pltpu.SemaphoreType.REGULAR,
            dma((4, 2)), dma((4,)), dma((4,)), dma((4,)), dma((4, 4)), dma((4, 4)), dma((4,)), dma((4,)),
            dma((4,)), dma((4,)), dma((4, 4)), dma((4, 4)), dma((4,)), dma((4,)), dma((4,)), dma((4,)),
        ],
        compiler_params=pltpu.CompilerParams(
            collective_id=0, has_side_effects=True, vmem_limit_bytes=60 << 20
        ),
        cost_estimate=pl.CostEstimate(flops=13 * 10**9, bytes_accessed=4 << 20, transcendentals=22 * 10**6),
        name="attend",
    )(doc_lengths, queries, keys, values)


def solution(mesh):
    rows = P(("outer", "inner"), None)
    return jax.shard_map(
        body, mesh=mesh, in_specs=(rows, rows, rows, P()), out_specs=rows, check_vma=False
    )
```

time: 89 us -> 72.9 us (0.82)
  Pallas kernels: 86.6 us -> 69.9 us
    pallas_call x1, Pallas kernels: 86.6 us -> 69.9 us  [body(): pl.pallas_call(kernel, out_shape=jax.ShapeDtypeStruct(queries.shape, bf16...]
where the time goes in v3:
time: 72.9 us; the launch traced here: 72.2 us
  Pallas kernels  69.9 us (96%)
  local copies, waits for them, and re-layouts  2.29 us (3%)
    pallas_call x1, Pallas kernels, body(): pl.pallas_call(kernel, out_shape=jax.ShapeDtypeStruct(queries.shape, bf16...  69.9 us
    unnamed x1, local copies, waits for them, and re-layouts  2.29 us

profile of v3, /device:TPU:224, one launch (start us, length us, event | category | flops | bytes accessed | tf_op | source)
XLA Modules:
  0.0 72.2 jit_solution(2929880658007444896)
XLA Ops:
  0.0 69.9 %attend.1 = bf16[128,4096]{1,0:T(8,128)(2,1)} custom-call(s32[16]{0:T(128)} %lens.1, bf16[128,4096]{1,0:T(8,128)(2,1)} %q_hbm.1, bf16[128,512]{1,0:T(8,128)(2,1)} %k_hbm.1, bf16[128,512]{1,0:T(8,128)(2,1)} %v_hbm.1), custom_call_target="tpu_custom_call" | custom-call | flops 12999999488 | bytes 4194304 | tf_op jit(solution)/shard_map/attend/pallas_call | solution.py:362
  69.9 2.3 %copy.6 = bf16[128,4096]{1,0:T(8,128)(2,1)} copy(bf16[128,4096]{1,0:T(8,128)(2,1)} %attend.1) | data formatting | bytes 2097152

commit v4 on v3

--- a/solution.py
+++ b/solution.py
@@ -139,6 +139,10 @@
     def _():
         kv[1] = jnp.zeros(kv.shape[1:], kv.dtype)
 
+    def on_y(p, d):
+        part = (p, (z + d) % 4)
+        return remote(kv.at[(0, *part)], kv.at[(2, *part)], s_y.at[d, p], r_y.at[p], (o + 2, i))
+
     zs, hs = [], []
     for p in range(4):
         arrived(kv.at[0, p, z], r_x.at[p])
@@ -157,13 +161,17 @@
         def _():
             far.start()
 
+        @pl.when(send_near)
+        def _():
+            on_y(p, 0).start()
+
         for d in (1, 2, 3):
-            cp = remote(kv.at[0, p, z], kv.at[0, p, z], s_z.at[d, p], r_z.at[d, p], at(dz=d))
-            cp.start()
-            zs.append(cp)
-
-    def on_y(p):
-        return remote(kv.at[0, p], kv.at[2, p], s_y.at[p], r_y.at[p], (o + 2, i))
+            zs.append(remote(kv.at[0, p, z], kv.at[0, p, z], s_z.at[d, p], r_z.at[d, p], at(dz=d)))
+
+        @pl.when(jnp.logical_not(from_far) | (p < 2))
+        def _():
+            for cp in zs[3 * p:]:
+                cp.start()
 
     def on_w(p, d):
         if p < 2:
@@ -181,14 +189,19 @@
 
         @pl.when(from_far)
         def _():
-            for d in (1, 2, 3) if p < 2 else (0, 1, 2, 3):
+            for d in (1, 2, 3):
                 arrived(kv.at[2, p, mz], r_w.at[d, p])
 
+        @pl.when(from_far & (p >= 2))
+        def _():
+            arrived(kv.at[2, p, mz], r_w.at[0, p])
+
     ones = jnp.where(lax.broadcasted_iota(jnp.int32, (WIDE, D), 1) == 0, 1.0, 0.0).astype(jnp.bfloat16)
 
-    def keys_of(slot, first, size):
-        key_value = kv[slot, first // NARROW:(first + size) // NARROW].reshape(size, 2 * D)
-        mask = km[slot, first:first + size, :]
+    def keys_of(slot, piece, count=1):
+        size = count * NARROW
+        key_value = kv[slot, pl.ds(piece, count)].reshape(size, 2 * D)
+        mask = km[slot, pl.ds(pl.multiple_of(piece * NARROW, NARROW), size), :]
         keys = jnp.concatenate([key_value[:, :D], mask], axis=1)
         values = jnp.concatenate([key_value[:, D:], ones[:size]], axis=1)
         return keys, values
@@ -217,7 +230,7 @@
     )
     causal = jnp.where(ahead <= z * TOK, 0.0, -BIG)
 
-    def queries_in(d, carry):
+    def queries_in(d):
         j = (x - d + 4) % 4
         arrived(qin.at[j], r_q.at[j])
         qpos = o * BLOCK + (j * 4 + z) * TOK + lax.broadcasted_iota(jnp.int32, (TOK, D), 0)
@@ -226,7 +239,31 @@
             rows = pl.ds(pl.multiple_of(j * CHUNK + h * TOK, TOK), TOK)
             qa[rows, :D] = qin[j, :, h * D:(h + 1) * D]
             qa[rows, D:] = mine
-        return carry
+
+    def first_own(steps_back):
+        for d in steps_back:
+            queries_in(d)
+        keys, values = keys_of(0, 0)
+        todo = []
+        for d in steps_back:
+            j = (x - d + 4) % 4
+            bias = jnp.where(ahead <= j * NARROW + z * TOK, 0.0, -BIG)
+            for r in range(0, CHUNK, ROWS):
+                todo.append((pl.ds(pl.multiple_of(j * CHUNK + r, ROWS), ROWS), keys, values, bias))
+        steps(todo)
+
+    def hand_on(p):
+        @pl.when(from_far)
+        def _():
+            arrived(kv.at[2, p, mz], r_h.at[p])
+            for d in (1, 2, 3):
+                on_w(p, d).start()
+
+        @pl.when(relay)
+        def _():
+            arrived(held.at[p], r_h.at[p + 2])
+            for d in (0, 1, 2, 3):
+                on_w(p + 2, d).start()
 
     def own(p):
         for d in (1, 2, 3):
@@ -234,36 +271,32 @@
 
         @pl.when(send_near)
         def _():
-            on_y(p).start()
+            for d in (1, 2, 3):
+                on_y(p, d).start()
 
         @pl.when(c == 0)
         def _():
             give(p, 0).start()
 
         if p == 0:
-            lax.fori_loop(0, 4, queries_in, 0)
-        if p == 3:
+            hand_on(0)
+            first_own((0, 1, 3))
+            hand_on(1)
+
             @pl.when(from_far)
             def _():
-                for n in (0, 1):
-                    arrived(kv.at[2, n, mz], r_h.at[n])
-                    for d in (1, 2, 3):
-                        on_w(n, d).start()
-
-            @pl.when(relay)
-            def _():
-                for n in (2, 3):
-                    arrived(held.at[n - 2], r_h.at[n])
-                    for d in (0, 1, 2, 3):
-                        on_w(n, d).start()
-
-        keys, values = keys_of(0, p * NARROW, NARROW)
+                for cp in zs[6:]:
+                    cp.start()
+
+            first_own((2,))
+            return
+        keys, values = keys_of(0, p)
         todo = []
         for r in range(p * CHUNK, 4 * CHUNK, ROWS):
             todo.append((slice(r, r + ROWS), keys, values, causal if r < (p + 1) * CHUNK else None))
         steps(todo)
 
-    def earlier(p):
+    def wait_first(p):
         @pl.when(c == 0)
         def _():
             wait_old(p)
@@ -272,65 +305,101 @@
         def _():
             arrived(kv.at[1, p], r_c.at[p])
 
-        @pl.when((c == 1) & has_prev)
-        def _():
-            for n in {0: (), 1: (0,), 2: (1,), 3: (2, 3)}[p]:
-                wait_old(n)
-                give(n, 2).start()
-
-        keys, values = keys_of(2 - c, p * NARROW, NARROW)
+    def wait_second(p):
+        @pl.when((c == 0) & has_prev)
+        def _():
+            arrived(kv.at[1, p], r_c.at[p])
+
+    def earlier(n, carry):
+        second = (n == 2) | (n == 4)
+        p = jnp.where(n == 3, 2, jnp.where((n == 1) | (n == 4), 1, 0))
+
+        @pl.when((c == 1) & has_prev & (n >= 1))
+        def _():
+            wait_old(n - 1)
+            give(n - 1, 2).start()
+
+        @pl.when(second)
+        def _():
+            wait_second(p)
+
+        @pl.when(jnp.logical_not(second))
+        def _():
+            wait_first(p)
+
+        slot = jnp.where(second, 1 + c, 2 - c)
+        keys, values = keys_of(slot, p)
         steps([(slice(r, r + ROWS), keys, values, None) for r in range(0, 4 * CHUNK, ROWS)])
-
-    for p in range(4):
-        own(p)
-    for p in range(4):
-        earlier(p)
-
-    @pl.when((c == 0) & has_prev)
-    def _():
-        for p in range(4):
-            arrived(kv.at[1, p], r_c.at[p])
-
-    def send_out(d):
-        return remote(obuf.at[d], cols(out_hbm, x, PER * D), s_o.at[d], r_o.at[d], at(dx=d))
-
-    keep = pltpu.make_async_copy(obuf.at[0], cols(out_hbm, x, PER * D), r_o.at[0])
+        return carry
+
+    own(0)
+    own(1)
+    lax.fori_loop(0, jnp.where(from_far, 2, 1), earlier, 0)
+    own(2)
+    lax.fori_loop(jnp.where(from_far, 2, 1), 2, earlier, 0)
+    own(3)
+    lax.fori_loop(2, 5, earlier, 0)
+    wait_first(3)
+    wait_second(2)
+    wait_second(3)
+
+    half = PER * D // 2
+
+    def span(n, width):
+        return pl.ds(pl.multiple_of(n * width, width), width)
+
+    def send_out(d, h):
+        return remote(
+            obuf.at[d, :, span(h, half)], out_hbm.at[:, span(2 * x + h, half)],
+            s_o.at[d, h], r_o.at[d, h], at(dx=d),
+        )
+
+    def keep(h):
+        return pltpu.make_async_copy(
+            obuf.at[0, :, span(h, half)], out_hbm.at[:, span(2 * x + h, half)], r_o.at[0, h]
+        )
 
     def last(n, carry):
-        d = jnp.where(n == 0, 2, jnp.where(n == 1, 1, jnp.where(n == 2, 3, 0)))
-        base = ((x + d) % 4) * CHUNK
+        pairs = (
+            (jnp.where(n == 0, 2, jnp.where(n == 3, 0, 1)), jnp.where(n == 2, 1, 0)),
+            (jnp.where(n == 0, 2, jnp.where(n == 3, 0, 3)), jnp.where(n == 1, 0, 1)),
+        )
         todo = []
-        for first in range(0, BLOCK, WIDE):
-            keys, values = keys_of(1 + c, first, WIDE)
-            for r in range(0, CHUNK, ROWS):
-                todo.append((pl.ds(pl.multiple_of(base + r, ROWS), ROWS), keys, values, None))
+        for keys, values in (keys_of(1 + c, 2, 2), keys_of(2 - c, 3)):
+            for d, h in pairs:
+                todo.append((span(((x + d) % 4) * 2 + h, ROWS), keys, values, None))
         steps(todo)
-        for h in range(PER):
-            part = acc[pl.ds(pl.multiple_of(base + h * TOK, TOK), TOK), :]
-            obuf[d, :, h * D:(h + 1) * D] = (part[:, :D] / part[:, D:D + 1]).astype(jnp.bfloat16)
-
-        @pl.when(d > 0)
-        def _():
-            send_out(d).start()
-
-        @pl.when(d == 0)
-        def _():
-            keep.start()
+        for d, h in pairs:
+            base = ((x + d) % 4) * CHUNK + h * ROWS
+            for m in range(ROWS // TOK):
+                part = acc[pl.ds(pl.multiple_of(base + m * TOK, TOK), TOK), :]
+                to = pl.ds(pl.multiple_of(h * half + m * D, D), D)
+                obuf[d, :, to] = (part[:, :D] / part[:, D:D + 1]).astype(jnp.bfloat16)
+
+            @pl.when(d > 0)
+            def _():
+                send_out(d, h).start()
+
+            @pl.when(d == 0)
+            def _():
+                keep(h).start()
 
         return carry
 
     lax.fori_loop(0, 4, last, 0)
 
-    keep.wait()
-    for d in (1, 2, 3):
-        send_out(d).wait()
+    for h in (0, 1):
+        keep(h).wait()
+        for d in (1, 2, 3):
+            send_out(d, h).wait()
     for cp in xs + qs + zs:
         cp.wait_send()
 
     @pl.when(send_near)
     def _():
         for p in range(4):
-            on_y(p).wait_send()
+            for d in range(4):
+                on_y(p, d).wait_send()
 
     @pl.when(send_far)
     def _():
@@ -374,15 +443,15 @@
             pltpu.VMEM((4, TOK, PER * D), bf16),
             pltpu.VMEM((2, TOK, 2 * D), bf16),
             pltpu.SemaphoreType.REGULAR,
-            dma((4, 2)), dma((4,)), dma((4,)), dma((4,)), dma((4, 4)), dma((4, 4)), dma((4,)), dma((4,)),
-            dma((4,)), dma((4,)), dma((4, 4)), dma((4, 4)), dma((4,)), dma((4,)), dma((4,)), dma((4,)),
+            dma((4, 2)), dma((4,)), dma((4,)), dma((4,)), dma((4, 4)), dma((4, 4)), dma((4, 4)), dma((4,)),
+            dma((4,)), dma((4,)), dma((4, 4)), dma((4, 4)), dma((4,)), dma((4,)), dma((4, 2)), dma((4, 2)),
         ],
         compiler_params=pltpu.CompilerParams(
-            collective_id=0, has_side_effects=True, vmem_limit_bytes=60 << 20
+            collective_id=0, has_side_effects=True, vmem_limit_bytes=48 << 20
         ),
         cost_estimate=pl.CostEstimate(flops=13 * 10**9, bytes_accessed=4 << 20, transcendentals=22 * 10**6),
         name="attend",
-    )(doc_lengths, queries, keys, values)
+    )(doc_lengths, *(pltpu.with_memory_space_constraint(a, pltpu.HBM) for a in (queries, keys, values)))
 
 
 def solution(mesh):

time: 72.9 us -> 71.4 us (0.979)
  Pallas kernels: 69.9 us -> 68.8 us
    pallas_call x1, Pallas kernels: 69.9 us -> 68.8 us  [body(): pl.pallas_call(kernel, out_shape=jax.ShapeDtypeStruct(queries.shape, bf16...]
    unnamed x1 -> x3, local copies, waits for them, and re-layouts: 2.29 us -> 1.63 us
where the time goes in v4:
time: 71.4 us; the launch traced here: 70.4 us
  Pallas kernels  68.8 us (96%)
  local copies, waits for them, and re-layouts  1.63 us (2%)
    pallas_call x1, Pallas kernels, body(): pl.pallas_call(kernel, out_shape=jax.ShapeDtypeStruct(queries.shape, bf16...  68.8 us
    unnamed x3, local copies, waits for them, and re-layouts  1.63 us

profile of v4, /device:TPU:224, one launch (start us, length us, event | category | flops | bytes accessed | tf_op | source)
XLA Modules:
  0.0 70.4 jit_solution(7913264110668131343)
XLA Ops:
  0.0 0.0 copy-start
  0.0 0.7 copy-done
  0.7 68.8 %attend.1 = bf16[128,4096]{1,0:T(8,128)(2,1)S(1)} custom-call(s32[16]{0:T(128)S(1)} %copy-done, bf16[128,4096]{1,0:T(8,128)(2,1)} %q_hbm.1, bf16[128,512]{1,0:T(8,128)(2,1)} %k_hbm.1, bf16[128,512]{1,0:T(8,128)(2,1)} %v_hbm.1), custom_call_target="tpu_custom_call" | custom-call | flops 12999999488 | bytes 4194304 | tf_op jit(solution)/shard_map/attend/pallas_call | solution.py:431
  69.5 1.0 %copy.6 = bf16[128,4096]{1,0:T(8,128)(2,1)} copy(bf16[128,4096]{1,0:T(8,128)(2,1)S(1)} %attend.1) | data formatting | bytes 2097152
Async XLA Ops:
  0.0 0.7 copy-start
